TPU v7x, 256 devices: a whole 4x4x8 slice. The times are simulated.
256 devices in a mesh: region: 4 (over y), shard: 64 (over x, z, core).
Axes of the slice: x: 4, y: 4, z: 8, core: 2. Of those that a mesh axis runs over, the one named last changes fastest.
Arguments:
- features: bfloat16 [65536, 1024], P(('region', 'shard')), may hold values from -6 to 6
- proj_weight: bfloat16 [1024, 1024], replicated, may hold values from -0.1875 to 0.1875
- proj_bias: float32 [1024], replicated, may hold values from -3 to 3
- self_weight: bfloat16 [1024, 1024], replicated, may hold values from -0.1875 to 0.1875
- nbr_weight: bfloat16 [1024, 1024], replicated, may hold values from -0.1875 to 0.1875
- out_bias: float32 [1024], replicated, may hold values from -3 to 3
- nbr_ids: int32 [65536, 8], P(('region', 'shard')), may hold values from 0 to 16383, as said below
- nbr_counts: int32 [65536, 8], P(('region', 'shard')), may hold values from 1 to 32
- live_slots: int32 [512], P(('region', 'shard')), may hold values from 1 to 8
- query_ids: int32 [16384], P(('region', 'shard')), may hold values from 0 to 255
- positive_ids: int32 [16384], P(('region', 'shard')), may hold values from 0 to 255
- neg_blocks: int32 [256, 4], P(('region', 'shard')), may hold values from 0 to 7, as said below
Outputs:
- embedding: bfloat16 [65536, 1024], P(('region', 'shard'))
- hinge_terms: float32 [16384, 4], P(('region', 'shard'))
Inputs may be any that keep to these rules, and one draw needn't show every extreme that they name: `nbr_ids`: entries index items of the item's own region. Of the 2048 neighbour slots of one device, at most 64 name items held by any one device, and exactly 64 name the items of one device. `neg_blocks`: entry g names block g % 2 of the device at the same shard index in region g // 2; never a block of the device's own region.
All inputs are finite; a program needn't handle non-finite values.
Results may differ from a plain program's by a relative error of at most 0.0036.
Values may be sent and summed in bfloat16 or wider, within the bound.
A program may use at most 128 MiB of HBM per device.

v0:
```python
import jax
import jax.numpy as jnp
from jax import lax
from jax.sharding import PartitionSpec as P

score_scale = 32.0
margin_value = 1.0
norm_eps = 1e-06


def body(
    features,
    proj_weight,
    proj_bias,
    self_weight,
    nbr_weight,
    out_bias,
    nbr_ids,
    nbr_counts,
    live_slots,
    query_ids,
    positive_ids,
    neg_blocks,
):
    item_dev = features.shape[0]
    hidden = proj_weight.shape[1]
    fanout = nbr_ids.shape[1]
    block_rows = item_dev // live_slots.shape[0]
    shards = lax.axis_size("shard")
    live_item = jnp.repeat(live_slots, block_rows, total_repeat_length=item_dev)
    slot_weight = jnp.where(
        jnp.arange(fanout, dtype=jnp.int32)[None, :] < live_item[:, None], nbr_counts, 0
    )
    weight_sum = jnp.sum(slot_weight.astype(jnp.float32), axis=1, keepdims=True)
    flat_ids = nbr_ids.reshape(-1)
    owners = flat_ids // item_dev
    local_row = flat_ids % item_dev
    slots = flat_ids.shape[0]
    capacity = max(2, 2 * slots // shards)
    onehot = (owners[:, None] == jnp.arange(shards, dtype=jnp.int32)[None, :]).astype(jnp.int32)
    before = jnp.cumsum(onehot, axis=0) - onehot
    slot_rank = jnp.take_along_axis(before, owners[:, None], axis=1)[:, 0]
    requests = jnp.zeros((shards, capacity), jnp.int32).at[owners, slot_rank].set(local_row)
    wanted = lax.all_to_all(requests, "shard", split_axis=0, concat_axis=0, tiled=True)
    outgoing = jnp.take(features, wanted, axis=0)
    incoming = lax.all_to_all(outgoing, "shard", split_axis=0, concat_axis=0, tiled=True)
    gathered = incoming[owners, slot_rank]
    slot_proj = jnp.maximum(
        jnp.dot(gathered, proj_weight, preferred_element_type=jnp.float32) + proj_bias, 0.0
    ).astype(jnp.bfloat16)
    slot_proj = slot_proj.reshape(item_dev, fanout, hidden)
    summed = jnp.einsum(
        "ik,ikh->ih",
        slot_weight.astype(jnp.bfloat16),
        slot_proj,
        preferred_element_type=jnp.float32,
    )
    aggregate = (summed / weight_sum).astype(jnp.bfloat16)
    activation = (
        jnp.dot(features, self_weight, preferred_element_type=jnp.float32)
        + jnp.dot(aggregate, nbr_weight, preferred_element_type=jnp.float32)
        + out_bias
    )
    activation = jnp.maximum(activation, 0.0)
    embedding = (
        activation * lax.rsqrt(jnp.mean(activation * activation, axis=-1, keepdims=True) + norm_eps)
    ).astype(jnp.bfloat16)
    query_emb = jnp.take(embedding, query_ids, axis=0)
    positive_emb = jnp.take(embedding, positive_ids, axis=0)
    neg_lists = neg_blocks[0]
    positive_score = (
        score_scale
        / hidden
        * jnp.sum(query_emb.astype(jnp.float32) * positive_emb.astype(jnp.float32), axis=-1)
    )
    start_value = jnp.zeros((query_emb.shape[0], neg_lists.shape[0]), jnp.float32)
    scores = (
        score_scale
        / hidden
        * jnp.dot(
            query_emb,
            lax.all_gather(embedding, "region", axis=0, tiled=True).T,
            preferred_element_type=jnp.float32,
        )
    )
    hinge_all = jnp.maximum(scores - positive_score[:, None] + margin_value, 0.0)
    block_mean = jnp.mean(hinge_all.reshape(query_emb.shape[0], -1, block_rows), axis=-1)
    pool_ids = jnp.int32(0) // block_rows + jnp.arange(block_mean.shape[1], dtype=jnp.int32)
    picked = jnp.where(
        neg_lists[None, :, None] == pool_ids[None, None, :], block_mean[:, None, :], 0.0
    )
    hinge_terms = start_value + jnp.sum(picked, axis=-1)
    return (embedding, hinge_terms)


def solution(mesh):
    in_specs = (
        P(("region", "shard"), None),
        P(),
        P(),
        P(),
        P(),
        P(),
        P(("region", "shard"), None),
        P(("region", "shard"), None),
        P(("region", "shard")),
        P(("region", "shard")),
        P(("region", "shard")),
        P(("region", "shard"), None),
    )
    out_specs = (P(("region", "shard"), None), P(("region", "shard"), None))
    return jax.shard_map(body, mesh=mesh, in_specs=in_specs, out_specs=out_specs, check_vma=False)
```

profile of v0, /device:TPU:1, one launch (start us, length us, event | category | flops | bytes accessed | tf_op | source)
XLA Modules:
  0.0 386.9 jit_solution(6796952247601897155)
XLA Ops:
  7.2 0.0 copy-start
  7.2 1.0 copy.39
  8.2 0.1 reshape.447
  8.3 0.1 reshape.449
  8.4 0.1 reshape.450
  8.5 0.1 reshape.446
  8.7 18.1 %reduce-window.14 = s32[64,16,128]{2,1,0:T(8,128)S(1)} reduce-window(s32[64,16,128]{2,1,0:T(8,128)S(1)} %fusion.15, s32[]{:T(128)} %constant.161.clone.1), window={size=1x1x128 pad=0_0x0_0x127_0}, to_apply=%region_0.1 | reduce-window | flops 16646144 | bytes 1048580 | tf_op jit(solution)/shard_map/reduce-window.3
  26.8 0.2 slice.37
  27.0 0.4 copy.48
  27.5 0.2 reduce-window.15
  27.6 0.2 broadcast_add_fusion
  28.0 0.2 fusion.13
  28.2 0.0 copy-start.5
  28.2 0.0 copy-start.1
  28.2 16.8 %gather_fusion.2 = s32[2048]{0:T(1024)S(1)} fusion(s32[2048,64]{0,1:T(8,128)S(1)} %fusion.13, s32[2048]{0:T(1024)S(1)} %bitcast.55), kind=kCustom, calls=%fused_computation.4 | custom fusion | bytes 32768 | tf_op jit(solution)/shard_map/jit(take_along_axis)/gather | solution.py:42
  45.0 0.1 shift-left_or_fusion
  45.1 0.1 and_reduce_fusion
  45.2 0.0 copy-done.5
  45.2 0.1 multiply_reduce_fusion.2
  45.3 8.1 %scatter_custom_fusion = s32[4096]{0:T(1024)S(1)} fusion(s32[2048]{0:T(1024)S(1)} %broadcast_select_fusion.3, s32[2048]{0:T(1024)S(1)} %get-tuple-element.18, s32[]{:T(128)} %constant.161.clone.1), kind=kCustom, calls=%fused_computation.69 | custom fusion | bytes 16388
  53.4 0.1 all_to_all.13
  53.4 22.1 %all_to_all.20 = s32[64,1,64]{2,1,0:T(1,128)S(1)} all-to-all(s32[64,1,64]{2,1,0:T(1,128)S(1)} %all_to_all.13), channel_id=1, replica_groups=mesh['region'=4,'shard'=64] {'shard'}, dimensions={0} | all-to-all | bytes 32768 | tf_op jit(solution)/shard_map/all_to_all | solution.py:44
  75.5 0.1 reshape.485
  75.6 0.0 copy-done.1
  75.7 18.3 %gather_fusion = bf16[4096,1024]{1,0:T(8,128)(2,1)} fusion(bf16[256,1024]{1,0:T(8,128)(2,1)S(1)} %copy-done.1, s32[4096]{0:T(1024)S(1)} %broadcast_clamp_fusion), kind=kCustom, calls=%fused_computation.2 | custom fusion | bytes 16793600 | tf_op jit(solution)/shard_map/jit(_take)/gather | solution.py:45
  93.9 7.3 %broadcast_select_fusion = bf16[64,64,1024]{2,1,0:T(8,128)(2,1)} fusion(bf16[64,64,1024]{2,1,0:T(8,128)(2,1)} %bitcast.56, pred[64,64]{1,0:T(8,128)(4,1)S(1)} %compare_and_fusion), kind=kLoop, calls=%fused_computation.7 | loop fusion | flops 4194304 | bytes 16781312 | tf_op jit(solution)/shard_map/jit(_take)/select_n | solution.py:45
  101.2 0.0 copy-start.4
  101.2 0.0 copy-start.3
  101.2 5.9 %all-to-all-start.1 = ((bf16[64,64,1024]{2,1,0:T(8,128)(2,1)}), bf16[64,64,1024]{2,1,0:T(8,128)(2,1)}, u32[]{:S(2)}, u32[]{:S(2)}) async-start(bf16[64,64,1024]{2,1,0:T(8,128)(2,1)} %broadcast_select_fusion), calls=%async_computation.1 | async-start | bytes 16777216 | tf_op jit(solution)/shard_map/all_to_all | solution.py:46
  107.1 0.2 all-gather.2.cloned.1.call-start
  107.4 0.0 copy-done.4
  107.4 0.6 fusion.32
  108.0 1.3 compare_select_fusion.12
  109.3 0.0 copy-done.3
  109.3 0.2 copy.46
  109.5 3.3 fusion.33
  112.8 180.1 %all-to-all-done.1 = bf16[64,64,1024]{2,1,0:T(8,128)(2,1)} async-done(((bf16[64,64,1024]{2,1,0:T(8,128)(2,1)}), bf16[64,64,1024]{2,1,0:T(8,128)(2,1)}, u32[]{:S(2)}, u32[]{:S(2)}) %all-to-all-start.1) | async-done | bytes 8388640 | tf_op jit(solution)/shard_map/all_to_all | solution.py:46
  292.9 0.0 copy-start.6
  292.9 40.8 %gather_fusion.1 = bf16[2048,1024]{1,0:T(8,128)(2,1)} fusion(bf16[64,64,1024]{2,1,0:T(8,128)(2,1)} %all-to-all-done.1, s32[2048]{0:T(1024)S(1)} %bitcast.54), kind=kCustom, calls=%fused_computation.3 | custom fusion | bytes 8404992 | tf_op jit(solution)/shard_map/gather | solution.py:47
  333.7 0.0 copy-done.6
  333.7 0.0 copy-start.2
  333.7 0.0 copy-start.7
  333.7 9.6 %fusion.1 = f32[256,1,1024]{2,1,0:T(1,128)} fusion(bf16[256,8,1]{1,2,0:T(2,128)(2,1)S(1)} %copy.46, f32[1024]{0:T(1024)S(1)} %copy-done.6, bf16[2048,1024]{1,0:T(8,128)(2,1)} %gather_fusion.1, bf16[1024,1024]{1,0:T(8,128)(2,1)} %param.17), kind=kOutput, calls=%fused_computation.9 | convolution fusion | flops 4305453056 | bytes 7348224 | tf_op jit(solution)/shard_map/ik,ikh->ih/dot_general | solution.py:52
  343.3 0.0 copy-done
  343.3 0.0 copy-done.2
  343.3 0.0 copy-done.7
  343.3 0.0 copy-start.8
  343.4 0.0 copy-start.9
  343.4 0.0 copy-start.10
  343.4 2.1 multiply_reduce_fusion
  345.5 0.9 multiply_convert_fusion
  346.5 0.0 all-gather.2.cloned.1.call-update
  346.5 0.0 copy-done.8
  346.5 0.0 copy-done.9
  346.6 0.0 copy-done.10
  346.6 0.1 iota_compare_fusion.3
  346.7 1.9 gather_fusion.3
  348.6 1.9 gather_fusion.4
  350.5 0.2 multiply_reduce_fusion.1
  350.7 26.0 %all-gather.2.cloned.1.call-done = bf16[1024,1024]{1,0:T(8,128)(2,1)} async-done(((bf16[256,1024]{1,0:T(8,128)(2,1)}), bf16[1024,1024]{1,0:T(8,128)(2,1)}) %all-gather.2.cloned.1.call-update) | async-done | bytes 2097168 | tf_op jit(solution)/shard_map/all_gather | solution.py:82
  376.7 2.4 fusion.10
  379.2 0.1 reduce_sum.48
  379.3 0.1 copy.45
  379.4 0.7 select_reduce_fusion
  (26 shorter events, 0.3 us)
Async XLA Ops:
  7.2 336.2 %copy-start = (bf16[1024,1024]{1,0:T(8,128)(2,1)S(1)}, bf16[1024,1024]{1,0:T(8,128)(2,1)}, u32[]{:S(2)}) copy-start(bf16[1024,1024]{1,0:T(8,128)(2,1)} %param.20) | copy-start | bytes 6291460
  28.2 17.0 %copy-start.5 = (s32[2]{0:T(128)S(1)}, s32[2]{0:T(128)}, u32[]{:S(2)}) copy-start(s32[2]{0:T(128)} %constant.179) | copy-start | bytes 28
  28.2 47.4 %copy-start.1 = (bf16[256,1024]{1,0:T(8,128)(2,1)S(1)}, bf16[256,1024]{1,0:T(8,128)(2,1)}, u32[]{:S(2)}) copy-start(bf16[256,1024]{1,0:T(8,128)(2,1)} %param.16) | copy-start | bytes 1572868
  101.2 6.2 %copy-start.4 = (s32[2]{0:T(128)S(1)}, s32[2]{0:T(128)}, u32[]{:S(2)}) copy-start(s32[2]{0:T(128)} %param.24) | copy-start | bytes 28
  101.2 8.1 %copy-start.3 = (s32[256,8]{0,1:T(8,128)S(1)}, s32[256,8]{0,1:T(8,128)}, u32[]{:S(2)}) copy-start(s32[256,8]{0,1:T(8,128)} %param.23) | copy-start | bytes 24580
  101.2 191.7 %all-to-all-start.1 = ((bf16[64,64,1024]{2,1,0:T(8,128)(2,1)}), bf16[64,64,1024]{2,1,0:T(8,128)(2,1)}, u32[]{:S(2)}, u32[]{:S(2)}) async-start(bf16[64,64,1024]{2,1,0:T(8,128)(2,1)} %broadcast_select_fusion), calls=%async_computation.1 | async-start | bytes 16777216 | tf_op jit(solution)/shard_map/all_to_all | solution.py:46
  107.1 269.6 %all-gather.2.cloned.1.call-start = ((), (), s32[]{:S(2)}) async-start(), calls=%async_computation.2 | async-start | bytes 2621440 | tf_op jit(solution)/shard_map/all_gather | solution.py:82
  292.9 40.8 %copy-start.6 = (f32[1024]{0:T(1024)S(1)}, f32[1024]{0:T(1024)}, u32[]{:S(2)}) copy-start(f32[1024]{0:T(1024)} %param.18) | copy-start | bytes 12292
  333.7 9.6 %copy-start.2 = (f32[256,1024]{1,0:T(8,128)S(1)}, f32[256,1024]{1,0:T(8,128)}, u32[]{:S(2)}) copy-start(f32[256,1024]{1,0:T(8,128)} %fusion.33) | copy-start | bytes 3145732
  333.7 9.6 %copy-start.7 = (f32[1024]{0:T(1024)S(1)}, f32[1024]{0:T(1024)}, u32[]{:S(2)}) copy-start(f32[1024]{0:T(1024)} %param.21) | copy-start | bytes 12292
  343.3 3.1 copy-start.8
  343.4 3.2 copy-start.9
  343.4 3.2 copy-start.10
Sparse Core Ops, SparseCore 0:
  346.6 30.1 all-gather.1
where the time goes:
time: 388 us; the launch traced here: 387 us
  waiting for transfers between devices  206 us (53%)
  local copies, waits for them, and re-layouts  90.8 us (23%)
  other arithmetic  29.9 us (8%)
  blocking collectives  22.1 us (6%)
  matrix products  17.4 us (4%)
  between operations  14.4 us (4%)
  starting transfers between devices  6.13 us (2%)
    all_to_all x1, waiting for transfers between devices, body(): lax.all_to_all(outgoing, 'shard', split_axis=0, concat_axis=0, tiled=True)  180 us
    gather x1, local copies, waits for them, and re-layouts, body(): gathered = incoming[owners, slot_rank]  40.8 us
    all_gather x1, waiting for transfers between devices, body(): lax.all_gather(embedding, 'region', axis=0, tiled=True)  26 us
    all_to_all x1, blocking collectives, body(): lax.all_to_all(requests, 'shard', split_axis=0, concat_axis=0, tiled=True)  22.1 us
    another operation x3, other arithmetic  18.5 us
    gather x1, local copies, waits for them, and re-layouts, body(): outgoing = jnp.take(features, wanted, axis=0)  18.3 us
    gather x1, local copies, waits for them, and re-layouts, body(): slot_rank = jnp.take_along_axis(before, owners[:, None], axis=1)[:, 0]  16.8 us
    dot_general x1, matrix products, body(): jnp.einsum('ik,ikh->ih', slot_weight.astype(jnp.bfloat16), slot_proj, pre...  9.62 us
  transfers between devices with their start and end apart: 2, of which 2 were waited for; matrix products, arithmetic and copies ran while one was open for 2% of the time, Pallas kernels for 0%

commit v1 on v0

--- a/solution.py
+++ b/solution.py
@@ -79,7 +79,10 @@
         / hidden
         * jnp.dot(
             query_emb,
-            lax.all_gather(embedding, "region", axis=0, tiled=True).T,
+            jnp.concatenate(
+                lax.all_to_all(jnp.stack([embedding] * lax.axis_size("region")), "region", 0, 0),
+                axis=0,
+            ).T,
             preferred_element_type=jnp.float32,
         )
     )

time: 388 us -> 376 us (0.969)
  between operations: 14.4 us -> 1.02 us
  starting transfers between devices: 6.13 us -> 10.4 us
    all_gather x1 -> x0, waiting for transfers between devices: 26 us -> none  [body(): lax.all_gather(embedding, 'region', axis=0, tiled=True)]
    all_to_all x0 -> x1, waiting for transfers between devices: none -> 24.9 us  [body(): lax.all_to_all(jnp.stack([embedding] * lax.axis_size('region')), 'region'...]
    all_to_all x0 -> x1, starting transfers between devices: none -> 4.44 us  [body(): lax.all_to_all(jnp.stack([embedding] * lax.axis_size('region')), 'region'...]
    unnamed x26 -> x28, local copies, waits for them, and re-layouts: 9.14 us -> 9.15 us
where the time goes in v1:
time: 376 us; the launch traced here: 375 us
  waiting for transfers between devices  205 us (55%)
  local copies, waits for them, and re-layouts  90 us (24%)
  other arithmetic  29.1 us (8%)
  blocking collectives  22.1 us (6%)
  matrix products  17.4 us (5%)
  starting transfers between devices  10.4 us (3%)
    all_to_all x1, waiting for transfers between devices, body(): lax.all_to_all(outgoing, 'shard', split_axis=0, concat_axis=0, tiled=True)  180 us
    gather x1, local copies, waits for them, and re-layouts, body(): gathered = incoming[owners, slot_rank]  40.8 us
    all_to_all x1, waiting for transfers between devices, body(): lax.all_to_all(jnp.stack([embedding] * lax.axis_size('region')), 'region'...  24.9 us
    all_to_all x1, blocking collectives, body(): lax.all_to_all(requests, 'shard', split_axis=0, concat_axis=0, tiled=True)  22.1 us
    another operation x3, other arithmetic  18.5 us
    gather x1, local copies, waits for them, and re-layouts, body(): outgoing = jnp.take(features, wanted, axis=0)  18.3 us
    gather x1, local copies, waits for them, and re-layouts, body(): slot_rank = jnp.take_along_axis(before, owners[:, None], axis=1)[:, 0]  16.8 us
    dot_general x1, matrix products, body(): jnp.einsum('ik,ikh->ih', slot_weight.astype(jnp.bfloat16), slot_proj, pre...  9.62 us
  transfers between devices with their start and end apart: 2, of which 2 were waited for; matrix products, arithmetic and copies ran while one was open for 2% of the time, Pallas kernels for 0%

profile of v1, /device:TPU:1, one launch (start us, length us, event | category | flops | bytes accessed | tf_op | source)
XLA Modules:
  0.0 375.2 jit_solution(739902140382473218)
XLA Ops:
  0.6 0.0 copy-start
  0.6 1.0 copy.39
  1.6 0.1 reshape.452
  1.7 0.1 reshape.454
  1.8 0.1 reshape.455
  2.0 0.1 reshape.451
  2.1 18.1 %reduce-window.14 = s32[64,16,128]{2,1,0:T(8,128)S(1)} reduce-window(s32[64,16,128]{2,1,0:T(8,128)S(1)} %fusion.15, s32[]{:T(128)} %constant.161.clone.1), window={size=1x1x128 pad=0_0x0_0x127_0}, to_apply=%region_0.1 | reduce-window | flops 16646144 | bytes 1048580 | tf_op jit(solution)/shard_map/reduce-window.3
  20.3 0.2 slice.37
  20.5 0.4 copy.48
  20.9 0.2 reduce-window.15
  21.1 0.2 broadcast_add_fusion
  21.5 0.2 fusion.13
  21.7 0.0 copy-start.6
  21.7 0.0 copy-start.1
  21.7 16.8 %gather_fusion.2 = s32[2048]{0:T(1024)S(1)} fusion(s32[2048,64]{0,1:T(8,128)S(1)} %fusion.13, s32[2048]{0:T(1024)S(1)} %bitcast.56), kind=kCustom, calls=%fused_computation.4 | custom fusion | bytes 32768 | tf_op jit(solution)/shard_map/jit(take_along_axis)/gather | solution.py:42
  38.5 0.1 shift-left_or_fusion
  38.6 0.1 and_reduce_fusion
  38.6 0.0 copy-done.6
  38.6 0.1 multiply_reduce_fusion.2
  38.8 8.1 %scatter_custom_fusion = s32[4096]{0:T(1024)S(1)} fusion(s32[2048]{0:T(1024)S(1)} %broadcast_select_fusion.3, s32[2048]{0:T(1024)S(1)} %get-tuple-element.18, s32[]{:T(128)} %constant.161.clone.1), kind=kCustom, calls=%fused_computation.69 | custom fusion | bytes 16388
  46.8 0.1 all_to_all.16
  46.9 22.1 %all_to_all.25 = s32[64,1,64]{2,1,0:T(1,128)S(1)} all-to-all(s32[64,1,64]{2,1,0:T(1,128)S(1)} %all_to_all.16), channel_id=1, replica_groups=mesh['region'=4,'shard'=64] {'shard'}, dimensions={0} | all-to-all | bytes 32768 | tf_op jit(solution)/shard_map/all_to_all | solution.py:44
  69.0 0.1 reshape.491
  69.1 0.0 copy-done.1
  69.1 18.3 %gather_fusion = bf16[4096,1024]{1,0:T(8,128)(2,1)} fusion(bf16[256,1024]{1,0:T(8,128)(2,1)S(1)} %copy-done.1, s32[4096]{0:T(1024)S(1)} %broadcast_clamp_fusion), kind=kCustom, calls=%fused_computation.2 | custom fusion | bytes 16793600 | tf_op jit(solution)/shard_map/jit(_take)/gather | solution.py:45
  87.4 7.3 %broadcast_select_fusion = bf16[64,64,1024]{2,1,0:T(8,128)(2,1)} fusion(bf16[64,64,1024]{2,1,0:T(8,128)(2,1)} %bitcast.57, pred[64,64]{1,0:T(8,128)(4,1)S(1)} %compare_and_fusion), kind=kLoop, calls=%fused_computation.7 | loop fusion | flops 4194304 | bytes 16781312 | tf_op jit(solution)/shard_map/jit(_take)/select_n | solution.py:45
  94.7 0.0 copy-start.5
  94.7 0.0 copy-start.4
  94.7 5.9 %all-to-all-start.1 = ((bf16[64,64,1024]{2,1,0:T(8,128)(2,1)}), bf16[64,64,1024]{2,1,0:T(8,128)(2,1)}, u32[]{:S(2)}, u32[]{:S(2)}) async-start(bf16[64,64,1024]{2,1,0:T(8,128)(2,1)} %broadcast_select_fusion), calls=%async_computation.1 | async-start | bytes 16777216 | tf_op jit(solution)/shard_map/all_to_all | solution.py:46
  100.6 0.0 copy-done.5
  100.6 0.6 fusion.32
  101.2 1.3 compare_select_fusion.12
  102.5 0.0 copy-done.4
  102.6 0.2 copy.46
  102.7 3.3 fusion.33
  106.0 180.3 %all-to-all-done.1 = bf16[64,64,1024]{2,1,0:T(8,128)(2,1)} async-done(((bf16[64,64,1024]{2,1,0:T(8,128)(2,1)}), bf16[64,64,1024]{2,1,0:T(8,128)(2,1)}, u32[]{:S(2)}, u32[]{:S(2)}) %all-to-all-start.1) | async-done | bytes 8388640 | tf_op jit(solution)/shard_map/all_to_all | solution.py:46
  286.4 0.0 copy-start.7
  286.4 40.8 %gather_fusion.1 = bf16[2048,1024]{1,0:T(8,128)(2,1)} fusion(bf16[64,64,1024]{2,1,0:T(8,128)(2,1)} %all-to-all-done.1, s32[2048]{0:T(1024)S(1)} %bitcast.55), kind=kCustom, calls=%fused_computation.3 | custom fusion | bytes 8404992 | tf_op jit(solution)/shard_map/gather | solution.py:47
  327.2 0.0 copy-done.7
  327.2 9.6 %fusion.1 = f32[256,1,1024]{2,1,0:T(1,128)} fusion(bf16[256,8,1]{1,2,0:T(2,128)(2,1)S(1)} %copy.46, f32[1024]{0:T(1024)S(1)} %copy-done.7, bf16[2048,1024]{1,0:T(8,128)(2,1)} %gather_fusion.1, bf16[1024,1024]{1,0:T(8,128)(2,1)} %param.17), kind=kOutput, calls=%fused_computation.9 | convolution fusion | flops 4305453056 | bytes 7348224 | tf_op jit(solution)/shard_map/ik,ikh->ih/dot_general | solution.py:52
  336.8 0.0 copy-done
  336.8 0.0 copy-done.3
  336.8 0.0 copy-done.8
  336.8 2.1 multiply_reduce_fusion
  338.9 0.0 copy-start.9
  338.9 0.0 copy-start.10
  339.0 0.0 copy-start.11
  339.0 0.1 multiply_convert_fusion
  339.1 0.0 copy-start.2
  339.1 1.6 stack.2
  340.7 4.4 %all-to-all-start.2 = ((bf16[4,256,1024]{2,1,0:T(8,128)(2,1)}), bf16[4,256,1024]{2,1,0:T(8,128)(2,1)}, u32[]{:S(2)}, u32[]{:S(2)}) async-start(bf16[4,256,1024]{2,1,0:T(8,128)(2,1)} %stack.2), calls=%async_computation.2 | async-start | bytes 4194304 | tf_op jit(solution)/shard_map/all_to_all | solution.py:83
  345.1 0.0 copy-done.9
  345.2 0.0 copy-done.10
  345.2 0.0 copy-done.11
  345.2 0.1 iota_compare_fusion.3
  345.3 0.7 gather_fusion.3
  346.0 0.7 gather_fusion.4
  346.7 0.0 copy-done.2
  346.7 0.2 multiply_reduce_fusion.1
  347.0 24.9 %all-to-all-done.2 = bf16[4,256,1024]{2,1,0:T(8,128)(2,1)} async-done(((bf16[4,256,1024]{2,1,0:T(8,128)(2,1)}), bf16[4,256,1024]{2,1,0:T(8,128)(2,1)}, u32[]{:S(2)}, u32[]{:S(2)}) %all-to-all-start.2) | async-done | bytes 2097184 | tf_op jit(solution)/shard_map/all_to_all | solution.py:83
  371.9 2.4 fusion.10
  374.3 0.1 reduce_sum.48
  374.4 0.1 copy.45
  374.5 0.7 select_reduce_fusion
  (28 shorter events, 0.4 us)
Async XLA Ops:
  0.6 336.2 %copy-start = (bf16[1024,1024]{1,0:T(8,128)(2,1)S(1)}, bf16[1024,1024]{1,0:T(8,128)(2,1)}, u32[]{:S(2)}) copy-start(bf16[1024,1024]{1,0:T(8,128)(2,1)} %param.20) | copy-start | bytes 6291460
  21.7 17.0 %copy-start.6 = (s32[2]{0:T(128)S(1)}, s32[2]{0:T(128)}, u32[]{:S(2)}) copy-start(s32[2]{0:T(128)} %constant.179) | copy-start | bytes 28
  21.7 47.4 %copy-start.1 = (bf16[256,1024]{1,0:T(8,128)(2,1)S(1)}, bf16[256,1024]{1,0:T(8,128)(2,1)}, u32[]{:S(2)}) copy-start(bf16[256,1024]{1,0:T(8,128)(2,1)} %param.16) | copy-start | bytes 1572868
  94.7 6.0 %copy-start.5 = (s32[2]{0:T(128)S(1)}, s32[2]{0:T(128)}, u32[]{:S(2)}) copy-start(s32[2]{0:T(128)} %param.24) | copy-start | bytes 28
  94.7 7.9 %copy-start.4 = (s32[256,8]{0,1:T(8,128)S(1)}, s32[256,8]{0,1:T(8,128)}, u32[]{:S(2)}) copy-start(s32[256,8]{0,1:T(8,128)} %param.23) | copy-start | bytes 24580
  94.7 191.7 %all-to-all-start.1 = ((bf16[64,64,1024]{2,1,0:T(8,128)(2,1)}), bf16[64,64,1024]{2,1,0:T(8,128)(2,1)}, u32[]{:S(2)}, u32[]{:S(2)}) async-start(bf16[64,64,1024]{2,1,0:T(8,128)(2,1)} %broadcast_select_fusion), calls=%async_computation.1 | async-start | bytes 16777216 | tf_op jit(solution)/shard_map/all_to_all | solution.py:46
  286.4 40.8 %copy-start.7 = (f32[1024]{0:T(1024)S(1)}, f32[1024]{0:T(1024)}, u32[]{:S(2)}) copy-start(f32[1024]{0:T(1024)} %param.18) | copy-start | bytes 12292
  327.2 9.6 %copy-start.3 = (f32[256,1024]{1,0:T(8,128)S(1)}, f32[256,1024]{1,0:T(8,128)}, u32[]{:S(2)}) copy-start(f32[256,1024]{1,0:T(8,128)} %fusion.33) | copy-start | bytes 3145732
  327.2 9.6 %copy-start.8 = (f32[1024]{0:T(1024)S(1)}, f32[1024]{0:T(1024)}, u32[]{:S(2)}) copy-start(f32[1024]{0:T(1024)} %param.21) | copy-start | bytes 12292
  338.9 6.2 %copy-start.9 = (s32[64]{0:T(128)S(1)}, s32[64]{0:T(128)}, u32[]{:S(2)}) copy-start(s32[64]{0:T(128)} %param.25) | copy-start | bytes 772
  338.9 6.2 %copy-start.10 = (s32[64]{0:T(128)S(1)}, s32[64]{0:T(128)}, u32[]{:S(2)}) copy-start(s32[64]{0:T(128)} %param.26) | copy-start | bytes 772
  339.0 6.3 %copy-start.11 = (s32[1,4]{1,0:T(1,128)S(1)}, s32[1,4]{1,0:T(1,128)}, u32[]{:S(2)}) copy-start(s32[1,4]{1,0:T(1,128)} %param.27) | copy-start | bytes 52
  339.1 7.6 %copy-start.2 = (bf16[256,1024]{1,0:T(8,128)(2,1)}, bf16[256,1024]{1,0:T(8,128)(2,1)S(1)}, u32[]{:S(2)}) copy-start(bf16[256,1024]{1,0:T(8,128)(2,1)S(1)} %multiply_convert_fusion) | copy-start | bytes 1572868
  340.7 31.2 %all-to-all-start.2 = ((bf16[4,256,1024]{2,1,0:T(8,128)(2,1)}), bf16[4,256,1024]{2,1,0:T(8,128)(2,1)}, u32[]{:S(2)}, u32[]{:S(2)}) async-start(bf16[4,256,1024]{2,1,0:T(8,128)(2,1)} %stack.2), calls=%async_computation.2 | async-start | bytes 4194304 | tf_op jit(solution)/shard_map/all_to_all | solution.py:83
